TPU v7x, 128 devices: a whole 4x4x4 slice. The times are simulated.
128 devices in a mesh: net: 8 (over z, core), strip: 16 (over y, x).
Axes of the slice: x: 4, y: 4, z: 4, core: 2. Of those that a mesh axis runs over, the one named last changes fastest.
Arguments:
- cond_charge: bfloat16 [3072, 32, 128], P(('net', 'strip')), may hold values from -6 to 6
- cond_live: int32 [128], P(('net', 'strip')), may hold values from 2 to 24, as said below
- near_src: int32 [3072, 16], P(('net', 'strip')), may hold values from -1 to 3071, as said below
- near_mat: bfloat16 [3072, 16, 128, 128], P(('net', 'strip')), may hold values from -0.125 to 0.125
- cond_basis: bfloat16 [3072, 16, 128], P(('net', 'strip')), may hold values from -0.5 to 0.5
- cond_rank: int32 [3072], P(('net', 'strip')), may hold values from 8 to 16
- far_src: int32 [3072, 16], P(('net', 'strip')), may hold values from -1 to 3583, as said below
- far_mat: bfloat16 [3072, 16, 16, 16], P(('net', 'strip')), may hold values from -0.375 to 0.375
- iface_charge: bfloat16 [512, 32, 128], P('strip', 'net'), may hold values from -6 to 6
- iface_near: bfloat16 [512, 3, 128, 128], P('strip'), may hold values from -0.3125 to 0.3125
- iface_basis: bfloat16 [512, 16, 128], P('strip'), may hold values from -0.5 to 0.5
- iface_rank: int32 [512], P('strip'), may hold values from 8 to 16
- iface_far_src: int32 [512, 16], P('strip'), may hold values from -1 to 3583, as said below
- iface_far_mat: bfloat16 [512, 16, 16, 16], P('strip'), may hold values from -0.375 to 0.375
Outputs:
- cond_pot: bfloat16 [3072, 32, 128], P(('net', 'strip'))
- iface_pot: bfloat16 [512, 32, 128], P('strip', 'net')
Inputs may be any that keep to these rules, and one draw needn't show every extreme that they name: `cond_live`: in every draw, two devices of every net group have all 24 slots live; live slots are the first ones of a device. `near_src`: entry 0 of a row is the row's own block. Every other entry is -1 (padding, only after the used entries) or a live conductor slot of a device with the same net index as the row's device. `far_src`: each entry is -1 (padding, only after the used entries), a live conductor slot, or an interface block number. `iface_far_src`: each entry is -1 (padding, only after the used entries), a live conductor slot, or an interface block number.
All inputs are finite; a program needn't handle non-finite values.
Results may differ from a plain program's by a relative error of at most 0.0027.
Values may be sent and summed in bfloat16 or wider, within the bound.
No kernel may reach another device: no remote copies, remote signals or barrier semaphores. Data moves between devices by JAX's collectives and lax.ppermute only.
A program may use at most 128 MiB of HBM per device.

v0:
```python
import jax
import jax.numpy as jnp
from jax import lax
from jax.sharding import PartitionSpec as P


def extended(array, sides, width):
    for axis, dim in sides:
        peers, length = (lax.axis_size(axis), array.shape[dim])
        up = [(i, (i + 1) % peers) for i in range(peers - 1)]
        down = [(j, i) for i, j in up]
        last = lax.slice_in_dim(array, length - width, length, axis=dim)
        leading = lax.slice_in_dim(array, 0, width, axis=dim)
        before = lax.ppermute(last, axis, up)
        after = lax.ppermute(leading, axis, down)
        array = jnp.concatenate([before, array, after], axis=dim)
    return array


def coeffs(block_basis, charge, block_rank):
    product = jnp.einsum("tap,trp->tar", block_basis, charge, preferred_element_type=jnp.float32)
    keep_rows = (jnp.arange(block_basis.shape[1])[None, :] < block_rank[:, None]).astype(
        jnp.float32
    )
    return (product * keep_rows[:, :, None]).astype(jnp.bfloat16)


def far_field(source_ids, far_mats, block_basis, block_rank, coef_table):
    usable = (source_ids >= 0).astype(jnp.bfloat16)
    fetched = coef_table[jnp.maximum(source_ids, 0)] * usable[:, :, None, None]
    gathered_far = jnp.einsum(
        "tkab,tkbr->tar", far_mats, fetched, preferred_element_type=jnp.float32
    )
    keep_rows = (jnp.arange(block_basis.shape[1])[None, :] < block_rank[:, None]).astype(
        jnp.float32
    )
    gathered_far = (gathered_far * keep_rows[:, :, None]).astype(jnp.bfloat16)
    return jnp.einsum("tap,tar->trp", block_basis, gathered_far, preferred_element_type=jnp.float32)


def shards(
    cond_charge,
    cond_live,
    near_src,
    near_mat,
    cond_basis,
    cond_rank,
    far_src,
    far_mat,
    iface_charge,
    iface_near,
    iface_basis,
    iface_rank,
    iface_far_src,
    iface_far_mat,
):
    cond_blocks = cond_charge.shape[0]
    iface_blocks = iface_charge.shape[0]
    excite_rows = iface_charge.shape[1]
    strip_count = lax.axis_size("strip")
    net_index = lax.axis_index("net")
    grouped = lax.all_gather(cond_charge, "strip", axis=0, tiled=True)
    local_ids = near_src - net_index * strip_count * cond_blocks
    usable = (near_src >= 0).astype(jnp.bfloat16)
    fetched = grouped[jnp.clip(local_ids, 0, grouped.shape[0] - 1)] * usable[:, :, None, None]
    near_part = jnp.einsum("tkpq,tkrq->trp", near_mat, fetched, preferred_element_type=jnp.float32)
    rimmed = extended(iface_charge, (("strip", 0),), 1)
    iface_near_part = jnp.einsum(
        "tpq,trq->trp", iface_near[:, 0], rimmed[:iface_blocks], preferred_element_type=jnp.float32
    )
    iface_near_part = iface_near_part + jnp.einsum(
        "tpq,trq->trp",
        iface_near[:, 1],
        rimmed[1 : iface_blocks + 1],
        preferred_element_type=jnp.float32,
    )
    iface_near_part = iface_near_part + jnp.einsum(
        "tpq,trq->trp", iface_near[:, 2], rimmed[2:], preferred_element_type=jnp.float32
    )
    cond_coef = coeffs(cond_basis, cond_charge, cond_rank)
    iface_local = coeffs(iface_basis, iface_charge, iface_rank)
    iface_full = lax.all_gather(iface_local, "net", axis=2, tiled=True)
    cond_table = lax.all_gather(cond_coef, ("net", "strip"), axis=0, tiled=True)
    iface_table = lax.all_gather(iface_full, "strip", axis=0, tiled=True)
    coef_table = jnp.concatenate([cond_table, iface_table], 0)
    cond_far = far_field(far_src, far_mat, cond_basis, cond_rank, coef_table)
    excite_table = lax.dynamic_slice_in_dim(coef_table, net_index * excite_rows, excite_rows, 2)
    iface_far = far_field(iface_far_src, iface_far_mat, iface_basis, iface_rank, excite_table)
    alive_mask = (jnp.arange(cond_blocks) < cond_live[0]).astype(jnp.float32)
    cond_pot = ((near_part + cond_far) * alive_mask[:, None, None]).astype(jnp.bfloat16)
    iface_pot = (iface_near_part + iface_far).astype(jnp.bfloat16)
    return (cond_pot, iface_pot)


def solution(mesh):
    placed = (
        P(("net", "strip"), None, None),
        P(("net", "strip")),
        P(("net", "strip"), None),
        P(("net", "strip"), None, None, None),
        P(("net", "strip"), None, None),
        P(("net", "strip")),
        P(("net", "strip"), None),
        P(("net", "strip"), None, None, None),
        P("strip", "net", None),
        P("strip", None, None, None),
        P("strip", None, None),
        P("strip"),
        P("strip", None),
        P("strip", None, None, None),
    )
    return jax.shard_map(
        shards,
        mesh=mesh,
        in_specs=placed,
        out_specs=(P(("net", "strip"), None, None), P("strip", "net", None)),
        check_vma=False,
    )
```

profile of v0, /device:TPU:0, one launch (start us, length us, event | category | flops | bytes accessed | tf_op | source)
XLA Modules:
  0.0 213.5 jit_solution(11559196575613654127)
XLA Ops:
  8.7 1.8 fusion.19
  11.3 1.3 collective-permute-start.1
  12.6 4.5 %collective-permute-start = (bf16[1,4,128]{2,1,0:T(4,128)(2,1)S(1)}, bf16[1,4,128]{2,1,0:T(4,128)(2,1)S(1)}, u32[]{:S(2)}, u32[]{:S(2)}) collective-permute-start(bf16[1,4,128]{2,1,0:T(4,128)(2,1)S(1)} %get-tuple-element.2), channel_id=1, source_target_pairs={{0,1},{1,2},{2,3},{3,4},{4,5},{5,6},{6,7},{7,8},{8,9},{9,10},{10,1... | collective-permute-start | bytes 3080 | tf_op jit(solution)/shard_map/ppermute | solution.py:14
  17.2 0.7 fusion.49
  17.9 0.9 fusion.27
  18.9 14.0 %all_gather.14 = bf16[32,16,32]{0,1,2:T(8,128)(2,1)S(1)} all-gather(bf16[32,16,4]{0,1,2:T(8,128)(2,1)S(1)} %copy.71), channel_id=1, replica_groups=mesh['net'=8,'strip'=16] {'net'}, dimensions={2}, use_global_device_ids=true | all-gather | bytes 36864 | tf_op jit(solution)/shard_map/all_gather | solution.py:82
  36.5 35.7 %all_gather.15 = bf16[512,16,32]{2,1,0:T(8,128)(2,1)} all-gather(bf16[32,16,32]{2,1,0:T(8,128)(2,1)S(1)} %copy.72), channel_id=1, replica_groups=mesh['net'=8,'strip'=16] {'strip'}, dimensions={0}, use_global_device_ids=true | all-gather | bytes 557056 | tf_op jit(solution)/shard_map/all_gather | solution.py:84
  72.3 1.9 fusion.31
  74.3 4.4 %copy.84 = bf16[32,16,16,16]{2,1,3,0:T(8,128)(2,1)} copy(bf16[32,16,16,16]{0,3,2,1:T(8,128)(2,1)S(1)} %copy-done.4) | data formatting | bytes 524288 | tf_op args[13]
  78.7 3.5 %copy.75 = bf16[24,16,16,16]{3,2,1,0:T(8,128)(2,1)} copy(bf16[24,16,16,16]{0,3,2,1:T(8,128)(2,1)S(1)} %copy-done.5) | data formatting | bytes 393216 | tf_op args[7]
  82.2 1.9 fusion.29
  84.1 3.1 %gather_fusion = bf16[384,32,128]{2,1,0:T(8,128)(2,1)S(1)} fusion(bf16[384,32,128]{2,1,0:T(8,128)(2,1)} %all-gather.3.cloned.1.call-done, s32[1024]{0:T(1024)S(1)} %pad_clamp_fusion.2), kind=kCustom, calls=%fused_computation | custom fusion | bytes 6292992 | tf_op jit(solution)/shard_map/gather | solution.py:65
  87.3 8.0 %fusion.6 = f32[24,32,128]{2,1,0:T(8,128)} fusion(bf16[24,16,128,128]{3,2,1,0:T(8,128)(2,1)} %param.17, bf16[24,16,32,128]{3,2,1,0:T(8,128)(2,1)S(1)} %bitcast.52, bf16[24,16]{1,0:T(8,128)(2,1)S(1)} %copy.70), kind=kOutput, calls=%fused_computation.10 | convolution fusion | flops 404226048 | bytes 16122624 | tf_op jit(solution)/shard_map/tkpq,tkrq->trp/dot_general | solution.py:66
  95.2 47.9 %all-gather.5.cloned.1.call-done = bf16[3072,16,32]{2,1,0:T(8,128)(2,1)} async-done(((bf16[24,16,32]{2,1,0:T(8,128)(2,1)}), bf16[3072,16,32]{2,1,0:T(8,128)(2,1)}) %all-gather.5.cloned.1.call-update) | async-done | bytes 3145744 | tf_op jit(solution)/shard_map/all_gather | solution.py:83
  143.1 6.8 %constant_dynamic-update-slice_fusion.1 = bf16[3584,16,32]{2,1,0:T(8,128)(2,1)S(1)} fusion(bf16[3072,16,32]{2,1,0:T(8,128)(2,1)} %all-gather.5.cloned.1.call-done), kind=kLoop, calls=%fused_computation.58 | loop fusion | bytes 15728640
  150.5 5.2 %copy-done.1 = bf16[3584,16,32]{2,1,0:T(8,128)(2,1)} copy-done((bf16[3584,16,32]{2,1,0:T(8,128)(2,1)}, bf16[3584,16,32]{2,1,0:T(8,128)(2,1)S(1)}, u32[]{:S(2)}) %copy-start.1) | copy-done | bytes 3670040
  155.7 7.8 %constant_dynamic-slice_fusion = bf16[3584,16,4]{2,1,0:T(8,128)(2,1)} fusion(bf16[3584,16,32]{2,1,0:T(8,128)(2,1)S(1)} %constant_dynamic-update-slice_fusion, s32[]{:T(128)S(6)} %select_n.9), kind=kLoop, calls=%fused_computation.62 | loop fusion | bytes 917508 | tf_op jit(solution)/shard_map/dynamic_slice | solution.py:87
  163.5 24.0 %copy.80 = bf16[3584,16,4]{1,2,0:T(4,128)(2,1)} copy(bf16[3584,16,4]{2,1,0:T(8,128)(2,1)} %constant_dynamic-slice_fusion) | data formatting | bytes 917504 | tf_op jit(solution)/shard_map/dynamic_slice | solution.py:87
  187.5 3.5 %gather_fusion.2 = bf16[512,16,4]{1,2,0:T(4,128)(2,1)S(1)} fusion(bf16[3584,16,4]{1,2,0:T(4,128)(2,1)} %copy.80, s32[1024]{0:T(1024)S(1)} %pad_clamp_fusion), kind=kCustom, calls=%fused_computation.2 | custom fusion | bytes 133120 | tf_op jit(solution)/shard_map/gather | solution.py:30
  191.1 0.9 copy.88
  192.0 7.2 %gather_fusion.1 = bf16[384,16,32]{2,1,0:T(8,128)(2,1)} fusion(bf16[3584,16,32]{2,1,0:T(8,128)(2,1)} %copy-done.1, s32[1024]{0:T(1024)S(1)} %pad_clamp_fusion.1), kind=kCustom, calls=%fused_computation.1 | custom fusion | bytes 787968 | tf_op jit(solution)/shard_map/gather | solution.py:30
  199.3 3.9 %fusion.9 = bf16[24,32,128]{2,1,0:T(8,128)(2,1)} fusion(f32[24,32,128]{2,1,0:T(8,128)S(1)} %copy-done.6, bf16[24,16,128]{2,1,0:T(8,128)(2,1)S(1)} %copy-done.8, bf16[24,16,16,16]{3,2,1,0:T(8,128)(2,1)} %copy.75, bf16[24,16,16,32]{3,2,1,0:T(8,128)(2,1)} %bitcast.53, bf16[24,16]{1,0:T(8,128)(2,1)S(1)} %copy.74, f32[24]{0:T(128)S(1)} %compare_convert_fusion.3, ...), kind=kOutput, calls=%fused_computation.11 | convolution fusion | flops 10543104 | bytes 1280352 | tf_op jit(solution)/shard_map/tap,tar->trp/dot_general | solution.py:38
  203.2 0.9 fusion.28
  204.1 2.5 %fusion.25 = bf16[32,4,128]{2,1,0:T(4,128)(2,1)} fusion(f32[32,4,128]{2,1,0:T(4,128)S(1)} %fusion.28, f32[32,4,128]{2,1,0:T(4,128)S(1)} %fusion.29, f32[32,4,128]{2,1,0:T(4,128)S(1)} %fusion.31, bf16[32,3,128,128]{3,2,1,0:T(8,128)(2,1)} %param.23, bf16[32,4,128]{2,1,0:T(4,128)(2,1)S(1)} %copy-done.7, bf16[1,4,128]{2,1,0:T(4,128)(2,1)S(1)} %collective-permute-done), kind=kOutput, calls=%fused_computation.23 | convolution fusion | flops 4327424 | bytes 1311744 | tf_op jit(solution)/shard_map/tpq,trq->trp/dot_general | solution.py:68
  (55 shorter events, 6.0 us)
Async XLA Ops:
  7.2 10.7 %copy-start = (bf16[32,16,128]{2,1,0:T(8,128)(2,1)S(1)}, bf16[32,16,128]{2,1,0:T(8,128)(2,1)}, u32[]{:S(2)}) copy-start(bf16[32,16,128]{2,1,0:T(8,128)(2,1)} %param.24) | copy-start | bytes 393220
  7.2 65.1 %copy-start.7 = (bf16[32,4,128]{2,1,0:T(4,128)(2,1)S(1)}, bf16[32,4,128]{2,1,0:T(4,128)(2,1)}, u32[]{:S(2)}) copy-start(bf16[32,4,128]{2,1,0:T(4,128)(2,1)} %param.22) | copy-start | bytes 98308
  7.2 65.0 %copy-start.9 = (s32[32,16]{0,1:T(8,128)S(1)}, s32[32,16]{0,1:T(8,128)}, u32[]{:S(2)}) copy-start(s32[32,16]{0,1:T(8,128)} %param.26) | copy-start | bytes 6148
  7.2 65.0 %copy-start.11 = (s32[24,16]{0,1:T(8,128)S(1)}, s32[24,16]{0,1:T(8,128)}, u32[]{:S(2)}) copy-start(s32[24,16]{0,1:T(8,128)} %param.20) | copy-start | bytes 4612
  7.2 65.0 %copy-start.10 = (s32[24,16]{0,1:T(8,128)S(1)}, s32[24,16]{0,1:T(8,128)}, u32[]{:S(2)}) copy-start(s32[24,16]{0,1:T(8,128)} %param.16) | copy-start | bytes 4612
  7.2 67.0 %copy-start.4 = (bf16[32,16,16,16]{0,3,2,1:T(8,128)(2,1)S(1)}, bf16[32,16,16,16]{0,3,2,1:T(8,128)(2,1)}, u32[]{:S(2)}) copy-start(bf16[32,16,16,16]{0,3,2,1:T(8,128)(2,1)} %param.27) | copy-start | bytes 786436
  7.2 76.9 %all-gather.3.cloned.1.call-start = ((), (), s32[]{:S(2)}) async-start(), calls=%async_computation | async-start | bytes 3342336 | tf_op jit(solution)/shard_map/all_gather | solution.py:62
  8.0 135.1 %all-gather.5.cloned.1.call-start = ((), (), s32[]{:S(2)}) async-start(), calls=%async_computation.1 | async-start | bytes 12681216 | tf_op jit(solution)/shard_map/all_gather | solution.py:83
  11.3 70.9 %collective-permute-start.1 = (bf16[1,4,128]{2,1,0:T(4,128)(2,1)S(1)}, bf16[1,4,128]{2,1,0:T(4,128)(2,1)S(1)}, u32[]{:S(2)}, u32[]{:S(2)}) collective-permute-start(bf16[1,4,128]{2,1,0:T(4,128)(2,1)S(1)} %get-tuple-element.3), channel_id=1, source_target_pairs={{1,0},{2,1},{3,2},{4,3},{5,4},{6,5},{7,6},{8,7},{9,8},{10,9},{11,1... | collective-permute-start | bytes 3080 | tf_op jit(solution)/shard_map/ppermute | solution.py:15
  12.6 191.5 %collective-permute-start = (bf16[1,4,128]{2,1,0:T(4,128)(2,1)S(1)}, bf16[1,4,128]{2,1,0:T(4,128)(2,1)S(1)}, u32[]{:S(2)}, u32[]{:S(2)}) collective-permute-start(bf16[1,4,128]{2,1,0:T(4,128)(2,1)S(1)} %get-tuple-element.2), channel_id=1, source_target_pairs={{0,1},{1,2},{2,3},{3,4},{4,5},{5,6},{6,7},{7,8},{8,9},{9,10},{10,1... | collective-permute-start | bytes 3080 | tf_op jit(solution)/shard_map/ppermute | solution.py:14
  36.5 42.2 %copy-start.5 = (bf16[24,16,16,16]{0,3,2,1:T(8,128)(2,1)S(1)}, bf16[24,16,16,16]{0,3,2,1:T(8,128)(2,1)}, u32[]{:S(2)}) copy-start(bf16[24,16,16,16]{0,3,2,1:T(8,128)(2,1)} %param.21) | copy-start | bytes 589828
  95.2 54.7 %copy-start.2 = (bf16[512,16,32]{2,1,0:T(8,128)(2,1)S(1)}, bf16[512,16,32]{2,1,0:T(8,128)(2,1)}, u32[]{:S(2)}) copy-start(bf16[512,16,32]{2,1,0:T(8,128)(2,1)} %all_gather.15) | copy-start | bytes 1572868
  150.4 5.2 %copy-start.1 = (bf16[3584,16,32]{2,1,0:T(8,128)(2,1)}, bf16[3584,16,32]{2,1,0:T(8,128)(2,1)S(1)}, u32[]{:S(2)}) copy-start(bf16[3584,16,32]{2,1,0:T(8,128)(2,1)S(1)} %constant_dynamic-update-slice_fusion) | copy-start | bytes 11010052
  191.0 8.2 %copy-start.6 = (f32[24,32,128]{2,1,0:T(8,128)S(1)}, f32[24,32,128]{2,1,0:T(8,128)}, u32[]{:S(2)}) copy-start(f32[24,32,128]{2,1,0:T(8,128)} %fusion.6) | copy-start | bytes 1179652
  191.1 8.2 %copy-start.8 = (bf16[24,16,128]{2,1,0:T(8,128)(2,1)S(1)}, bf16[24,16,128]{2,1,0:T(8,128)(2,1)}, u32[]{:S(2)}) copy-start(bf16[24,16,128]{2,1,0:T(8,128)(2,1)} %param.18) | copy-start | bytes 294916
  199.3 4.0 %copy-start.3 = (bf16[32,16,16,16]{2,1,3,0:T(8,128)(2,1)S(1)}, bf16[32,16,16,16]{2,1,3,0:T(8,128)(2,1)}, u32[]{:S(2)}) copy-start(bf16[32,16,16,16]{2,1,3,0:T(8,128)(2,1)} %copy.84) | copy-start | bytes 786436
Sparse Core Ops, SparseCore 0:
  10.2 54.8 all-gather.2
  68.7 74.3 all-gather.4
where the time goes:
time: 215 us; the launch traced here: 213 us
  local copies, waits for them, and re-layouts  68.8 us (32%)
  blocking collectives  49.8 us (23%)
  waiting for transfers between devices  48.6 us (23%)
  matrix products  21.9 us (10%)
  between operations  15 us (7%)
  starting transfers between devices  5.9 us (3%)
  other arithmetic  3.64 us (2%)
    all_gather x1, waiting for transfers between devices, shards(): cond_table = lax.all_gather(cond_coef, ('net', 'strip'), axis=0, tiled=True)  47.9 us
    all_gather x1, blocking collectives, shards(): iface_table = lax.all_gather(iface_full, 'strip', axis=0, tiled=True)  35.7 us
    dynamic_slice x2, local copies, waits for them, and re-layouts, shards(): lax.dynamic_slice_in_dim(coef_table, net_index * excite_rows, excite_rows...  31.9 us
    unnamed x27, local copies, waits for them, and re-layouts  19.9 us
    all_gather x1, blocking collectives, shards(): iface_full = lax.all_gather(iface_local, 'net', axis=2, tiled=True)  14 us
    gather x3, local copies, waits for them, and re-layouts, far_field(): fetched = coef_table[jnp.maximum(source_ids, 0)] * usable[:, :, None, None]  11.7 us
    dot_general x1, matrix products, shards(): jnp.einsum('tkpq,tkrq->trp', near_mat, fetched, preferred_element_type=jn...  7.99 us
    dot_general x2, matrix products, far_field(): jnp.einsum('tap,tar->trp', block_basis, gathered_far, preferred_element_t...  4.8 us
  transfers between devices with their start and end apart: 4, of which 1 were waited for; matrix products, arithmetic and copies ran while one was open for 40% of the time, Pallas kernels for 0%

commit v1 on v0

v1 whole, which is shorter than its diff:
```python
import functools

import jax
import jax.numpy as jnp
from jax import lax
from jax.experimental import pallas as pl
from jax.experimental.pallas import tpu as pltpu
from jax.sharding import Mesh, PartitionSpec as P

ALL = ("z", "core", "y", "x")
BF, F32, I32 = jnp.bfloat16, jnp.float32, jnp.int32
CBD, IBD, R, RHS, NEAR, FAR = 24, 32, 16, 32, 16, 16
HALF = CBD // 2
ROWS = 120
SMEM = pl.BlockSpec(memory_space=pltpu.SMEM)
VMEM = pl.BlockSpec(memory_space=pltpu.VMEM)
ANY = pl.BlockSpec(memory_space=pl.ANY)


def exchange(dim0, mask0, dim1, mask1):
    pairs = []
    for d in range(128):
        z, c, y, x = d >> 5, (d >> 4) & 1, (d >> 2) & 3, d & 3
        dim, mask = (dim0, mask0) if c == 0 else (dim1, mask1)
        z ^= mask if dim == "z" else 0
        y ^= mask if dim == "y" else 0
        x ^= mask if dim == "x" else 0
        pairs.append((d, ((z * 2 + c) * 4 + y) * 4 + x))
    return pairs


A_STEPS = [("x", 1, "x", 3), ("x", 3, "x", 1), ("y", 1, "y", 3), ("y", 3, "y", 1)]
B_STEPS = [("y", 1, "y", 3), ("y", 3, "y", 1), ("x", 1, "x", 3), ("x", 3, "x", 1)]
PARTNER = [(d, d ^ 16) for d in range(128)]


def coef_kernel(crank, irank, cc, cb, ic, ib, out, pay, x4, sems):
    lane = lax.broadcasted_iota(I32, (R, 128), 1)
    row = lax.broadcasted_iota(I32, (R, 128), 0)
    nt = (((1,), (1,)), ((), ()))
    for g in range(CBD // 4):
        q = cc[4 * g : 4 * g + 4].reshape(4 * RHS, 128)
        b = cb[4 * g : 4 * g + 4].reshape(4 * R, 128)
        full = lax.dot_general(b, q, nt, preferred_element_type=F32)
        tile = jnp.zeros((R, 128), F32)
        for j in range(4):
            keep = (lane // RHS == j) & (row < crank[4 * g + j])
            tile = jnp.where(keep, full[R * j : R * j + R], tile)
        pay[R * g : R * g + R, :] = tile.astype(BF)
    for i in range(IBD):
        x4[4 * i : 4 * i + 4, :] = ic[i].astype(F32)
    x = x4[...].astype(BF)
    full = lax.dot_general(ib[...].reshape(IBD * R, 128), x, nt, preferred_element_type=F32)
    tile = jnp.zeros((R, 128), F32)
    for i in range(IBD):
        keep = (lane // 4 == i) & (row < irank[i])
        tile = jnp.where(keep, full[R * i : R * i + R], tile)
    pay[96:112, :] = tile.astype(BF)
    pay[112:120, :] = jnp.concatenate([x4[0:4, :], x4[124:128, :]], 0).astype(BF)
    copies = [pltpu.make_async_copy(pay, out.at[d], sems.at[d]) for d in range(64)]
    for copy in copies:
        copy.start()
    for copy in copies:
        copy.wait()


def coef_call(crank, irank, cc, cb, ic, ib):
    return pl.pallas_call(
        coef_kernel,
        out_shape=jax.ShapeDtypeStruct((64, ROWS, 128), BF),
        in_specs=[SMEM, SMEM, VMEM, VMEM, VMEM, VMEM],
        out_specs=ANY,
        scratch_shapes=[
            pltpu.VMEM((ROWS, 128), BF),
            pltpu.VMEM((128, 128), F32),
            pltpu.SemaphoreType.DMA((64,)),
        ],
        cost_estimate=pl.CostEstimate(flops=40_000_000, bytes_accessed=3_000_000, transcendentals=0),
        name="coefs",
    )(crank, irank, cc, cb, ic, ib)


def iface_near_kernel(ic, nm, out, x4):
    nt = (((1,), (1,)), ((), ()))
    blocks = nm.shape[0]
    step = pl.program_id(0)
    x4[0:8, :] = jnp.zeros((8, 128), F32)
    x4[136:144, :] = jnp.zeros((8, 128), F32)
    for i in range(IBD):
        x4[8 + 4 * i : 12 + 4 * i, :] = ic[i].astype(F32)
    for j in range(blocks):
        base = 8 + 4 * (step * blocks + j)
        acc = jnp.zeros((4, 128), F32)
        for m in range(3):
            x = x4[pl.ds(base + 4 * (m - 1), 4), :].astype(BF)
            acc = acc + lax.dot_general(x, nm[j, m], nt, preferred_element_type=F32)
        out[4 * j : 4 * j + 4, :] = acc


def iface_near_call(ic, nm):
    blocks = 8
    return pl.pallas_call(
        iface_near_kernel,
        grid=(IBD // blocks,),
        out_shape=jax.ShapeDtypeStruct((128, 128), F32),
        in_specs=[
            pl.BlockSpec((IBD, 4, 128), lambda i: (0, 0, 0)),
            pl.BlockSpec((blocks, 3, 128, 128), lambda i: (i, 0, 0, 0)),
        ],
        out_specs=pl.BlockSpec((4 * blocks, 128), lambda i: (i, 0)),
        scratch_shapes=[pltpu.VMEM((144, 128), F32)],
        cost_estimate=pl.CostEstimate(flops=50_000_000, bytes_accessed=6_000_000, transcendentals=0),
        name="iface_near",
    )(ic, nm)


def near_kernel(idx, a0, a1, b0, b1, nm, out, tab, sems):
    step = pl.program_id(0)
    blocks = nm.shape[0]

    @pl.when(step == 0)
    def _():
        copies = [
            pltpu.make_async_copy(src, tab.at[pl.ds(96 * i, 96)], sems.at[i])
            for i, src in enumerate((a0, a1, b0, b1))
        ]
        for copy in copies:
            copy.start()
        tab[384] = jnp.zeros((RHS, 128), BF)
        for copy in copies:
            copy.wait()

    for j in range(blocks):
        t = step * blocks + j
        x = jnp.concatenate([tab[idx[k, t]] for k in range(NEAR)], 1)
        w = jnp.concatenate([nm[j, k] for k in range(NEAR)], 1)
        out[j] = lax.dot_general(x, w, (((1,), (1,)), ((), ())), preferred_element_type=F32)


def near_call(idx, pieces, nm):
    blocks = 4
    return pl.pallas_call(
        near_kernel,
        grid=(CBD // blocks,),
        out_shape=jax.ShapeDtypeStruct((CBD, RHS, 128), F32),
        in_specs=[SMEM, ANY, ANY, ANY, ANY]
        + [pl.BlockSpec((blocks, NEAR, 128, 128), lambda i: (i, 0, 0, 0))],
        out_specs=pl.BlockSpec((blocks, RHS, 128), lambda i: (i, 0, 0)),
        scratch_shapes=[pltpu.VMEM((385, RHS, 128), BF), pltpu.SemaphoreType.DMA((4,))],
        cost_estimate=pl.CostEstimate(flops=400_000_000, bytes_accessed=20_000_000, transcendentals=0),
        name="near",
    )(idx, *pieces, nm)


def far_kernel(
    tile_c, lg_c, tile_i, lg_i, crank, irank, where_am_i, live,
    own, other, near, inear, fm, ifm, cb, ib, edge0, edge1, perm,
    cpot, ipot, tab, utab, gi, xi, sems,
):
    net, strip, core = where_am_i[0], where_am_i[1], where_am_i[2]
    mine = where_am_i[3]
    copies = [
        pltpu.make_async_copy(src, tab.at[i], sems.at[i]) for i, src in enumerate((own, other))
    ]
    for copy in copies:
        copy.start()
    lane = lax.broadcasted_iota(I32, (R, 128), 1)
    row = lax.broadcasted_iota(I32, (R, 128), 0)
    group = lane // RHS
    nt = (((1,), (1,)), ((), ()))
    tn = (((0,), (0,)), ((), ()))
    for copy in copies:
        copy.wait()
    for s in range(16):
        xi[R * s : R * s + R, :] = jnp.concatenate(
            [tab[jnp.bitwise_xor(n & 1, core), (n >> 1) * 16 + s, 96:112, :] for n in range(8)], 1
        )
    u = jnp.dot(xi[...], perm[...], preferred_element_type=F32).astype(BF)
    for s in range(16):
        for j in range(8):
            utab[s * 8 + j] = u[R * s : R * s + R, 128 * j : 128 * j + 128]

    def sums(tiles, groups, mats, t):
        parts = []
        for k in range(FAR):
            where, lg = tiles[k, t], groups[k, t]
            raw = utab[where]
            parts.append(jnp.where(group == lg, raw, jnp.zeros_like(raw)))
        stacked = jnp.concatenate(parts, 0)
        return jnp.dot(mats, stacked, preferred_element_type=F32)

    def fold(v):
        v = v + pltpu.roll(v, 64, 1)
        return v + pltpu.roll(v, 32, 1)

    zero = jnp.zeros((R, 128), F32)
    for d in range(128):
        for g in range(6):
            utab[128 + d * 6 + g] = tab[d // 64, d % 64, R * g : R * g + R, :]
    for q in range(CBD // 4):
        rows = []
        for j in range(4):
            t = 4 * q + j
            v = fold(sums(tile_c, lg_c, fm[t], t))
            rows.append(jnp.where((group == j) & (row < crank[t]), v, zero))
        gmat = jnp.concatenate(rows, 0).astype(BF)
        basis = cb[4 * q : 4 * q + 4].reshape(4 * R, 128)
        far = lax.dot_general(gmat, basis, tn, preferred_element_type=F32)
        for j in range(4):
            t = 4 * q + j
            alive = jnp.where(t < live[0], 1.0, 0.0)
            cpot[t] = ((near[t] + far[RHS * j : RHS * j + RHS]) * alive).astype(BF)
    for t in range(IBD):
        v = fold(sums(tile_i, lg_i, ifm[t], t))
        v = pltpu.roll(v, lax.rem(4 * t - 4 * net + 128, 128), 1)
        gi[R * t : R * t + R, :] = jnp.where((lane // 4 == t) & (row < irank[t]), v, zero).astype(BF)
    far = lax.dot_general(gi[...], ib[...].reshape(IBD * R, 128), tn, preferred_element_type=F32)
    total = far + inear[...]
    before = tab[0, jnp.maximum(mine - 1, 0), 112:120, :].astype(F32)
    after = tab[0, jnp.minimum(mine + 1, 63), 112:120, :].astype(F32)
    before = jnp.where(strip > 0, before, 0.0).astype(BF)
    after = jnp.where(strip < 15, after, 0.0).astype(BF)
    head = lax.dot_general(before, edge0[...], nt, preferred_element_type=F32)
    tail = lax.dot_general(after, edge1[...], nt, preferred_element_type=F32)
    for t in range(IBD):
        v = total[4 * t : 4 * t + 4]
        if t == 0:
            v = v + head[4:8]
        if t == IBD - 1:
            v = v + tail[0:4]
        ipot[t] = v.astype(BF)


def far_call(scalars, arrays):
    return pl.pallas_call(
        far_kernel,
        out_shape=(
            jax.ShapeDtypeStruct((CBD, RHS, 128), BF),
            jax.ShapeDtypeStruct((IBD, 4, 128), BF),
        ),
        in_specs=[SMEM] * 8 + [ANY, ANY] + [VMEM] * 9,
        out_specs=(VMEM, VMEM),
        scratch_shapes=[
            pltpu.VMEM((2, 64, ROWS, 128), BF),
            pltpu.VMEM((896, R, 128), BF),
            pltpu.VMEM((IBD * R, 128), BF),
            pltpu.VMEM((256, 1024), BF),
            pltpu.SemaphoreType.DMA((2,)),
        ],
        cost_estimate=pl.CostEstimate(flops=1_000_000_000, bytes_accessed=12_000_000, transcendentals=0),
        name="far",
    )(*scalars, *arrays)


def far_index(ids, core):
    dev, slot = ids // CBD, ids % CBD
    half = jnp.bitwise_xor((dev >> 4) & 1, core)
    dev64 = (dev >> 5) * 16 + (dev & 15)
    cond = 128 + (half * 64 + dev64) * 6 + (slot >> 2)
    i = ids - 128 * CBD
    iface = (i >> 5) * 8 + ((i & 31) >> 2)
    is_iface = ids >= 128 * CBD
    tile = jnp.where(is_iface, iface, cond)
    group = jnp.where(is_iface, i & 3, slot & 3)
    return jnp.where(ids < 0, 0, tile), jnp.where(ids < 0, -1, group)


def near_index(ids, core, y, x, net):
    local = ids - net * (16 * CBD)
    dev, slot = local // CBD, local % CBD

    def place(off):
        g = jnp.bitwise_xor(off, off >> 1)
        return jnp.where(core == 0, g, ((g & 1) << 1) | (g >> 1))

    py = place(jnp.bitwise_xor(dev >> 2, y))
    px = place(jnp.bitwise_xor(dev & 3, x))
    at_a = (py * 4 + px) * HALF + slot
    at_b = 192 + (px * 4 + py) * HALF + slot - HALF
    return jnp.where(ids < 0, 384, jnp.where(slot < HALF, at_a, at_b))


def shards(
    cond_charge, cond_live, near_src, near_mat, cond_basis, cond_rank, far_src, far_mat,
    iface_charge, iface_near, iface_basis, iface_rank, iface_far_src, iface_far_mat,
):
    z, core, y, x = (lax.axis_index(a) for a in ALL)
    net, strip = z * 2 + core, y * 4 + x
    swap = lambda v, step: lax.ppermute(v, ALL, exchange(*step))
    a, b = cond_charge[:HALF], cond_charge[HALF:]
    pieces = []
    for n, (sa, sb) in enumerate(zip(A_STEPS, B_STEPS)):
        ra, rb = swap(a, sa), swap(b, sb)
        if n == 3:
            pieces = [a, ra, b, rb]
        else:
            a, b = jnp.concatenate([a, ra], 0), jnp.concatenate([b, rb], 0)
    pay = coef_call(cond_rank, iface_rank, cond_charge, cond_basis, iface_charge, iface_basis)
    own = lax.all_to_all(pay, ("z", "y", "x"), 0, 0, tiled=True)
    other = lax.ppermute(own, ALL, PARTNER)
    inear = iface_near_call(iface_charge, iface_near)
    nidx = near_index(near_src.T, core, y, x, net)
    tile_c, lg_c = far_index(far_src.T, core)
    tile_i, lg_i = far_index(iface_far_src.T, core)
    fm = far_mat.transpose(0, 2, 1, 3).reshape(CBD, R, FAR * R)
    ifm = iface_far_mat.transpose(0, 2, 1, 3).reshape(IBD, R, FAR * R)
    r = lax.broadcasted_iota(I32, (1024, 1024), 0)
    c = lax.broadcasted_iota(I32, (1024, 1024), 1)
    target = ((r >> 4) & 7) * 128 + ((r >> 2) & 3) * 32 + (r >> 7) * 4 + (r & 3)
    perm = (c == target).astype(BF)
    near = near_call(nidx, pieces, near_mat)
    me = jnp.stack([net, strip, core, z * 16 + strip]).astype(I32)
    return far_call(
        (tile_c, lg_c, tile_i, lg_i, cond_rank, iface_rank, me, cond_live),
        (own, other, near, inear, fm, ifm, cond_basis, iface_basis,
         iface_near[0, 0], iface_near[IBD - 1, 2], perm),
    )


def solution(mesh):
    grid = Mesh(mesh.devices.reshape(4, 2, 4, 4), ALL)
    net, strip = ("z", "core"), ("y", "x")
    every = lambda n: P(ALL, *(None,) * (n - 1))
    by_strip = lambda n: P(strip, *(None,) * (n - 1))
    return jax.shard_map(
        shards,
        mesh=grid,
        in_specs=(
            every(3), every(1), every(2), every(4), every(3), every(1), every(2), every(4),
            P(strip, net, None), by_strip(4), by_strip(3), by_strip(1), by_strip(2), by_strip(4),
        ),
        out_specs=(every(3), P(strip, net, None)),
        check_vma=False,
    )
```

time: 215 us -> 104 us (0.48)
  local copies, waits for them, and re-layouts: 68.8 us -> 10.1 us
  blocking collectives: 49.8 us -> 0 us
  Pallas kernels: 0 us -> 27.3 us
  matrix products: 21.9 us -> 0 us
  starting transfers between devices: 5.9 us -> 21 us
  waiting for transfers between devices: 48.6 us -> 34.7 us
  between operations: 15 us -> 1.45 us
  other arithmetic: 3.64 us -> 8.34 us
    all_gather x2 -> x0, blocking collectives: 49.8 us -> none  [the longest x1 35.7 us: shards(): iface_table = lax.all_gather(iface_full, 'strip', axis=0, tiled=True)]
    all_gather x2 -> x0, waiting for transfers between devices: 47.9 us -> none  [the longest x1 47.9 us: shards(): cond_table = lax.all_gather(cond_coef, ('net', 'strip'), axis=0, tiled=True)]
    dynamic_slice x2 -> x0, local copies, waits for them, and re-layouts: 31.9 us -> none  [shards(): lax.dynamic_slice_in_dim(coef_table, net_index * excite_rows, excite_rows...]
    ppermute x2 -> x9, waiting for transfers between devices: 0.01 us -> 30.1 us  [the longest x8 30.1 us: shards(): swap = lambda v, step: lax.ppermute(v, ALL, exchange(*step))]
    pallas_call x0 -> x4, Pallas kernels: none -> 27.3 us  [the longest x1 11 us: near_call(): pl.pallas_call(near_kernel, grid=(CBD // blocks,), out_shape=jax.ShapeDty...]
    dot_general x8 -> x0, matrix products: 21.9 us -> none  [the longest x1 7.99 us: shards(): jnp.einsum('tkpq,tkrq->trp', near_mat, fetched, preferred_element_type=jn...]
    unnamed x27 -> x10, local copies, waits for them, and re-layouts: 19.9 us -> 0.03 us
    gather x4 -> x0, local copies, waits for them, and re-layouts: 14.8 us -> none  [the longest x3 11.7 us: far_field(): fetched = coef_table[jnp.maximum(source_ids, 0)] * usable[:, :, None, None]]
  transfers between devices with their start and end apart: 4 -> 10, of which waited for: 1 -> 4; matrix products, arithmetic and copies ran while one was open for 40% -> 18% of each run, Pallas kernels for 0% -> 15%
where the time goes in v1:
time: 104 us; the launch traced here: 103 us
  waiting for transfers between devices  34.7 us (33%)
  Pallas kernels  27.3 us (26%)
  starting transfers between devices  21 us (20%)
  local copies, waits for them, and re-layouts  10.1 us (10%)
  other arithmetic  8.34 us (8%)
  between operations  1.45 us (1%)
    ppermute x8, waiting for transfers between devices, shards(): swap = lambda v, step: lax.ppermute(v, ALL, exchange(*step))  30.1 us
    all_to_all x1, starting transfers between devices, shards(): own = lax.all_to_all(pay, ('z', 'y', 'x'), 0, 0, tiled=True)  11.7 us
    pallas_call x1, Pallas kernels, near_call(): pl.pallas_call(near_kernel, grid=(CBD // blocks,), out_shape=jax.ShapeDty...  11 us
    ppermute x8, starting transfers between devices, shards(): swap = lambda v, step: lax.ppermute(v, ALL, exchange(*step))  9.3 us
    pallas_call x1, Pallas kernels, far_call(): pl.pallas_call(far_kernel, out_shape=(jax.ShapeDtypeStruct((CBD, RHS, 128...  8.54 us
    all_to_all x1, waiting for transfers between devices, shards(): own = lax.all_to_all(pay, ('z', 'y', 'x'), 0, 0, tiled=True)  4.61 us
    pallas_call x1, Pallas kernels, iface_near_call(): pl.pallas_call(iface_near_kernel, grid=(IBD // blocks,), out_shape=jax.Sh...  4.56 us
    concatenate x6, other arithmetic, shards(): a, b = (jnp.concatenate([a, ra], 0), jnp.concatenate([b, rb], 0))  4.1 us
  transfers between devices with their start and end apart: 10, of which 4 were waited for; matrix products, arithmetic and copies ran while one was open for 18% of the time, Pallas kernels for 15%

profile of v1, /device:TPU:0, one launch (start us, length us, event | category | flops | bytes accessed | tf_op | source)
XLA Modules:
  0.0 102.9 jit_solution(15484140441576417447)
XLA Ops:
  0.6 3.3 %coefs.1 = bf16[64,120,128]{2,1,0:T(8,128)(2,1)} custom-call(s32[24]{0:T(128)} %crank.3, s32[32]{0:T(128)} %irank.3, bf16[24,32,128]{2,1,0:T(8,128)(2,1)} %cc.1, bf16[24,16,128]{2,1,0:T(8,128)(2,1)} %cb.3, bf16[32,4,128]{2,1,0:T(4,128)(2,1)} %ic.3, bf16[32,16,128]{2,1,0:T(8,128)(2,1)} %ib.3), custom_call_target="tpu_custom_call" | custom-call | flops 40000000 | bytes 3000000 | tf_op jit(solution)/shard_map/coefs/pallas_call | solution.py:68
  3.9 11.7 %all-to-all-start = ((bf16[64,120,128]{2,1,0:T(8,128)(2,1)}), bf16[64,120,128]{2,1,0:T(8,128)(2,1)S(1)}, u32[]{:S(2)}, u32[]{:S(2)}) async-start(bf16[64,120,128]{2,1,0:T(8,128)(2,1)} %coefs.1), calls=%async_computation | async-start | bytes 3932160 | tf_op jit(solution)/shard_map/all_to_all | solution.py:299
  15.6 1.7 %collective-permute-start.5 = (bf16[12,32,128]{2,1,0:T(8,128)(2,1)S(1)}, bf16[12,32,128]{2,1,0:T(8,128)(2,1)S(1)}, u32[]{:S(2)}, u32[]{:S(2)}) collective-permute-start(bf16[12,32,128]{2,1,0:T(8,128)(2,1)S(1)} %get-tuple-element.4), channel_id=1, source_target_pairs={{0,4},{1,5},{2,6},{3,7},{4,0},{5,1},{6,2},{7,3},{8,12},{9,13},{10,... | collective-permute-start | bytes 294920 | tf_op jit(solution)/shard_map/ppermute | solution.py:289
  17.3 1.5 %collective-permute-start.1 = (bf16[12,32,128]{2,1,0:T(8,128)(2,1)S(1)}, bf16[12,32,128]{2,1,0:T(8,128)(2,1)S(1)}, u32[]{:S(2)}, u32[]{:S(2)}) collective-permute-start(bf16[12,32,128]{2,1,0:T(8,128)(2,1)S(1)} %get-tuple-element.5), channel_id=1, source_target_pairs={{0,1},{1,0},{2,3},{3,2},{4,5},{5,4},{6,7},{7,6},{8,9},{9,8},{10,11... | collective-permute-start | bytes 294920 | tf_op jit(solution)/shard_map/ppermute | solution.py:289
  18.8 18.4 %collective-permute-done.5 = bf16[12,32,128]{2,1,0:T(8,128)(2,1)S(1)} collective-permute-done((bf16[12,32,128]{2,1,0:T(8,128)(2,1)S(1)}, bf16[12,32,128]{2,1,0:T(8,128)(2,1)S(1)}, u32[]{:S(2)}, u32[]{:S(2)}) %collective-permute-start.5) | collective-permute-done | bytes 98336 | tf_op jit(solution)/shard_map/ppermute | solution.py:289
  37.2 2.7 %collective-permute-start.6 = (bf16[24,32,128]{2,1,0:T(8,128)(2,1)S(1)}, bf16[24,32,128]{2,1,0:T(8,128)(2,1)S(1)}, u32[]{:S(2)}, u32[]{:S(2)}) collective-permute-start(bf16[24,32,128]{2,1,0:T(8,128)(2,1)S(1)} %pad_maximum_fusion.5), channel_id=1, source_target_pairs={{0,12},{1,13},{2,14},{3,15},{4,8},{5,9},{6,10},{7,11},{8,4},{9,5},... | collective-permute-start | bytes 589832 | tf_op jit(solution)/shard_map/ppermute | solution.py:289
  39.9 4.6 %all-to-all-done.own = bf16[64,120,128]{2,1,0:T(8,128)(2,1)S(1)} async-done(((bf16[64,120,128]{2,1,0:T(8,128)(2,1)}), bf16[64,120,128]{2,1,0:T(8,128)(2,1)S(1)}, u32[]{:S(2)}, u32[]{:S(2)}) %all-to-all-start) | async-done | bytes 1966112 | tf_op jit(solution)/shard_map/all_to_all | solution.py:299
  44.5 0.9 collective-permute-start.2
  45.5 0.6 select_select_fusion.idx
  46.1 5.4 %collective-permute-done.2 = bf16[24,32,128]{2,1,0:T(8,128)(2,1)S(1)} collective-permute-done((bf16[24,32,128]{2,1,0:T(8,128)(2,1)S(1)}, bf16[24,32,128]{2,1,0:T(8,128)(2,1)S(1)}, u32[]{:S(2)}, u32[]{:S(2)}) %collective-permute-start.2) | collective-permute-done | bytes 196640 | tf_op jit(solution)/shard_map/ppermute | solution.py:289
  51.5 0.9 collective-permute-start.3
  53.2 6.3 %collective-permute-done.3 = bf16[48,32,128]{2,1,0:T(8,128)(2,1)} collective-permute-done((bf16[48,32,128]{2,1,0:T(8,128)(2,1)S(1)}, bf16[48,32,128]{2,1,0:T(8,128)(2,1)}, u32[]{:S(2)}, u32[]{:S(2)}) %collective-permute-start.3) | collective-permute-done | bytes 393248 | tf_op jit(solution)/shard_map/ppermute | solution.py:289
  59.5 1.9 %pad_maximum_fusion.a0 = bf16[96,32,128]{2,1,0:T(8,128)(2,1)} fusion(bf16[48,32,128]{2,1,0:T(8,128)(2,1)} %collective-permute-done.3, bf16[24,32,128]{2,1,0:T(8,128)(2,1)S(1)} %collective-permute-done.2, bf16[12,32,128]{2,1,0:T(8,128)(2,1)S(1)} %collective-permute-done.1, bf16[12,32,128]{2,1,0:T(8,128)(2,1)S(1)} %get-tuple-element.5), kind=kLoop, calls=%fused_computation.2 | loop fusion | flops 1179648 | bytes 1572864 | tf_op jit(solution)/shard_map/concatenate | solution.py:297
  61.5 2.0 %pad_maximum_fusion.1.b0 = bf16[96,32,128]{2,1,0:T(8,128)(2,1)} fusion(bf16[48,32,128]{2,1,0:T(8,128)(2,1)} %collective-permute-done.7, bf16[24,32,128]{2,1,0:T(8,128)(2,1)S(1)} %collective-permute-done.6, bf16[12,32,128]{2,1,0:T(8,128)(2,1)S(1)} %collective-permute-done.5, bf16[12,32,128]{2,1,0:T(8,128)(2,1)S(1)} %get-tuple-element.4), kind=kLoop, calls=%fused_computation.3 | loop fusion | flops 1179648 | bytes 1572864 | tf_op jit(solution)/shard_map/concatenate | solution.py:297
  63.6 1.5 %collective-permute-start.8 = (bf16[96,32,128]{2,1,0:T(8,128)(2,1)}, bf16[96,32,128]{2,1,0:T(8,128)(2,1)}, u32[]{:S(2)}, u32[]{:S(2)}) collective-permute-start(bf16[96,32,128]{2,1,0:T(8,128)(2,1)} %pad_maximum_fusion.1.b0), channel_id=1, source_target_pairs={{0,3},{1,2},{2,1},{3,0},{4,7},{5,6},{6,5},{7,4},{8,11},{9,10},{10,... | collective-permute-start | bytes 2359304 | tf_op jit(solution)/shard_map/ppermute | solution.py:289
  66.4 1.5 %copy.19 = bf16[32,16,16,16]{0,3,2,1:T(8,128)(2,1)S(1)} copy(bf16[32,16,16,16]{0,3,1,2:T(8,128)(2,1)} %bitcast.118) | data formatting | bytes 524288 | tf_op jit(solution)/shard_map/transpose | solution.py:306
  67.9 1.2 %copy.20.ifm = bf16[32,16,256]{2,1,0:T(8,128)(2,1)} copy(bf16[32,16,256]{0,2,1:T(8,128)(2,1)S(1)} %bitcast.117) | data formatting | bytes 524288 | tf_op jit(solution)/shard_map/reshape | solution.py:306
  69.0 3.8 %copy.18 = bf16[24,16,16,16]{3,2,1,0:T(8,128)(2,1)S(1)} copy(bf16[24,16,16,16]{0,3,1,2:T(8,128)(2,1)} %bitcast.119) | data formatting | bytes 393216 | tf_op jit(solution)/shard_map/transpose | solution.py:305
  72.8 2.2 %reshape.10.fm = bf16[24,16,256]{2,1,0:T(8,128)(2,1)} reshape(bf16[24,16,16,16]{3,2,1,0:T(8,128)(2,1)S(1)} %copy.18) | data formatting | bytes 393216 | tf_op jit(solution)/shard_map/reshape | solution.py:305
  75.0 4.6 %iface_near.1.inear = f32[128,128]{1,0:T(8,128)} custom-call(bf16[32,4,128]{2,1,0:T(4,128)(2,1)} %ic.3, bf16[32,3,128,128]{3,2,1,0:T(8,128)(2,1)} %nm.3), custom_call_target="tpu_custom_call" | custom-call | flops 50000000 | bytes 6000000 | tf_op jit(solution)/shard_map/iface_near/pallas_call | solution.py:102
  80.2 1.4 %slice_bitcast_fusion = (bf16[128,128]{1,0:T(8,128)(2,1)}, bf16[128,128]{1,0:T(8,128)(2,1)}) fusion(bf16[32,3,128,128]{3,2,1,0:T(8,128)(2,1)} %nm.3), kind=kLoop, calls=%fused_computation.8 | loop fusion | bytes 131072 | tf_op jit(solution)/shard_map/squeeze | solution.py:316
  81.6 1.7 %fusion.perm = bf16[1024,1024]{1,0:T(8,128)(2,1)} fusion(s32[1024]{0:T(1024)S(1)} %fusion.18), kind=kLoop, calls=%fused_computation.1 | loop fusion | flops 2097152 | bytes 2101248 | tf_op jit(solution)/shard_map/convert_element_type | solution.py:310
  83.3 11.0 %near.1 = f32[24,32,128]{2,1,0:T(8,128)} custom-call(s32[16,24]{1,0:T(8,128)} %select_select_fusion.idx, bf16[96,32,128]{2,1,0:T(8,128)(2,1)} %pad_maximum_fusion.a0, bf16[96,32,128]{2,1,0:T(8,128)(2,1)} %collective-permute-done.4.a1, bf16[96,32,128]{2,1,0:T(8,128)(2,1)} %pad_maximum_fusion.1.b0, bf16[96,32,128]{2,1,0:T(8,128)(2,1)} %collective-permute-done.8.b1, ...), custom_call_target="tpu_custom_call" | custom-call | flops 400000000 | bytes 20000000 | tf_op jit(solution)/shard_map/near/pallas_call | solution.py:142
  94.3 8.5 %far.1 = (bf16[24,32,128]{2,1,0:T(8,128)(2,1)}, bf16[32,4,128]{2,1,0:T(4,128)(2,1)}) custom-call(s32[16,24]{1,0:T(8,128)} %get-tuple-element.9.tile_c, s32[16,24]{1,0:T(8,128)} %get-tuple-element.8.lg_c, s32[16,32]{1,0:T(8,128)} %get-tuple-element.7.tile_i, s32[16,32]{1,0:T(8,128)} %get-tuple-element.6.lg_i, s32[24]{0:T(128)} %crank.3, s32[32]{0:T(128)} %irank.3, ...), custom_call_target="tpu_custom_call" | custom-call | flops 1000000000 | bytes 12000000 | tf_op jit(solution)/shard_map/far/pallas_call | solution.py:235
  (28 shorter events, 2.2 us)
Async XLA Ops:
  3.9 11.7 %copy-start.1 = (bf16[24,32,128]{2,1,0:T(8,128)(2,1)S(1)}, bf16[24,32,128]{2,1,0:T(8,128)(2,1)}, u32[]{:S(2)}) copy-start(bf16[24,32,128]{2,1,0:T(8,128)(2,1)} %cc.1) | copy-start | bytes 589828
  3.9 41.6 %copy-start.4 = (s32[24,16]{0,1:T(8,128)S(1)}, s32[24,16]{0,1:T(8,128)}, u32[]{:S(2)}) copy-start(s32[24,16]{0,1:T(8,128)} %param.16) | copy-start | bytes 4612
  3.9 40.6 %all-to-all-start = ((bf16[64,120,128]{2,1,0:T(8,128)(2,1)}), bf16[64,120,128]{2,1,0:T(8,128)(2,1)S(1)}, u32[]{:S(2)}, u32[]{:S(2)}) async-start(bf16[64,120,128]{2,1,0:T(8,128)(2,1)} %coefs.1), calls=%async_computation | async-start | bytes 3932160 | tf_op jit(solution)/shard_map/all_to_all | solution.py:299
  15.6 37.0 %copy-start.2 = (s32[24,16]{0,1:T(8,128)S(1)}, s32[24,16]{0,1:T(8,128)}, u32[]{:S(2)}) copy-start(s32[24,16]{0,1:T(8,128)} %param.20) | copy-start | bytes 4612
  15.6 21.5 %collective-permute-start.5 = (bf16[12,32,128]{2,1,0:T(8,128)(2,1)S(1)}, bf16[12,32,128]{2,1,0:T(8,128)(2,1)S(1)}, u32[]{:S(2)}, u32[]{:S(2)}) collective-permute-start(bf16[12,32,128]{2,1,0:T(8,128)(2,1)S(1)} %get-tuple-element.4), channel_id=1, source_target_pairs={{0,4},{1,5},{2,6},{3,7},{4,0},{5,1},{6,2},{7,3},{8,12},{9,13},{10,... | collective-permute-start | bytes 294920 | tf_op jit(solution)/shard_map/ppermute | solution.py:289
  17.3 27.2 %collective-permute-start.1 = (bf16[12,32,128]{2,1,0:T(8,128)(2,1)S(1)}, bf16[12,32,128]{2,1,0:T(8,128)(2,1)S(1)}, u32[]{:S(2)}, u32[]{:S(2)}) collective-permute-start(bf16[12,32,128]{2,1,0:T(8,128)(2,1)S(1)} %get-tuple-element.5), channel_id=1, source_target_pairs={{0,1},{1,0},{2,3},{3,2},{4,5},{5,4},{6,7},{7,6},{8,9},{9,8},{10,11... | collective-permute-start | bytes 294920 | tf_op jit(solution)/shard_map/ppermute | solution.py:289
  37.2 15.2 %collective-permute-start.6 = (bf16[24,32,128]{2,1,0:T(8,128)(2,1)S(1)}, bf16[24,32,128]{2,1,0:T(8,128)(2,1)S(1)}, u32[]{:S(2)}, u32[]{:S(2)}) collective-permute-start(bf16[24,32,128]{2,1,0:T(8,128)(2,1)S(1)} %pad_maximum_fusion.5), channel_id=1, source_target_pairs={{0,12},{1,13},{2,14},{3,15},{4,8},{5,9},{6,10},{7,11},{8,4},{9,5},... | collective-permute-start | bytes 589832 | tf_op jit(solution)/shard_map/ppermute | solution.py:289
  44.5 19.1 %copy-start = (bf16[64,120,128]{2,1,0:T(8,128)(2,1)}, bf16[64,120,128]{2,1,0:T(8,128)(2,1)S(1)}, u32[]{:S(2)}) copy-start(bf16[64,120,128]{2,1,0:T(8,128)(2,1)S(1)} %all-to-all-done.own) | copy-start | bytes 5898244
  44.5 49.8 %collective-permute-start = (bf16[64,120,128]{2,1,0:T(8,128)(2,1)S(1)}, bf16[64,120,128]{2,1,0:T(8,128)(2,1)}, u32[]{:S(2)}, u32[]{:S(2)}) collective-permute-start(bf16[64,120,128]{2,1,0:T(8,128)(2,1)S(1)} %all-to-all-done.own), channel_id=1, source_target_pairs={{0,16},{1,17},{2,18},{3,19},{4,20},{5,21},{6,22},{7,23},{8,24},{9,... | collective-permute-start | bytes 5898248 | tf_op jit(solution)/shard_map/ppermute | solution.py:300
  44.5 7.0 %collective-permute-start.2 = (bf16[24,32,128]{2,1,0:T(8,128)(2,1)S(1)}, bf16[24,32,128]{2,1,0:T(8,128)(2,1)S(1)}, u32[]{:S(2)}, u32[]{:S(2)}) collective-permute-start(bf16[24,32,128]{2,1,0:T(8,128)(2,1)S(1)} %pad_maximum_fusion.4), channel_id=1, source_target_pairs={{0,3},{1,2},{2,1},{3,0},{4,7},{5,6},{6,5},{7,4},{8,11},{9,10},{10,... | collective-permute-start | bytes 589832 | tf_op jit(solution)/shard_map/ppermute | solution.py:289
  51.5 8.0 %collective-permute-start.3 = (bf16[48,32,128]{2,1,0:T(8,128)(2,1)S(1)}, bf16[48,32,128]{2,1,0:T(8,128)(2,1)}, u32[]{:S(2)}, u32[]{:S(2)}) collective-permute-start(bf16[48,32,128]{2,1,0:T(8,128)(2,1)S(1)} %pad_maximum_fusion.2), channel_id=1, source_target_pairs={{0,4},{1,5},{2,6},{3,7},{4,0},{5,1},{6,2},{7,3},{8,12},{9,13},{10,... | collective-permute-start | bytes 1179656 | tf_op jit(solution)/shard_map/ppermute | solution.py:289
  52.5 9.1 %collective-permute-start.7 = (bf16[48,32,128]{2,1,0:T(8,128)(2,1)S(1)}, bf16[48,32,128]{2,1,0:T(8,128)(2,1)}, u32[]{:S(2)}, u32[]{:S(2)}) collective-permute-start(bf16[48,32,128]{2,1,0:T(8,128)(2,1)S(1)} %pad_maximum_fusion.3), channel_id=1, source_target_pairs={{0,1},{1,0},{2,3},{3,2},{4,5},{5,4},{6,7},{7,6},{8,9},{9,8},{10,11... | collective-permute-start | bytes 1179656 | tf_op jit(solution)/shard_map/ppermute | solution.py:289
  61.4 21.9 %collective-permute-start.4 = (bf16[96,32,128]{2,1,0:T(8,128)(2,1)}, bf16[96,32,128]{2,1,0:T(8,128)(2,1)}, u32[]{:S(2)}, u32[]{:S(2)}) collective-permute-start(bf16[96,32,128]{2,1,0:T(8,128)(2,1)} %pad_maximum_fusion.a0), channel_id=1, source_target_pairs={{0,12},{1,13},{2,14},{3,15},{4,8},{5,9},{6,10},{7,11},{8,4},{9,5},... | collective-permute-start | bytes 2359304 | tf_op jit(solution)/shard_map/ppermute | solution.py:289
  63.6 19.8 %collective-permute-start.8 = (bf16[96,32,128]{2,1,0:T(8,128)(2,1)}, bf16[96,32,128]{2,1,0:T(8,128)(2,1)}, u32[]{:S(2)}, u32[]{:S(2)}) collective-permute-start(bf16[96,32,128]{2,1,0:T(8,128)(2,1)} %pad_maximum_fusion.1.b0), channel_id=1, source_target_pairs={{0,3},{1,2},{2,1},{3,0},{4,7},{5,6},{6,5},{7,4},{8,11},{9,10},{10,... | collective-permute-start | bytes 2359304 | tf_op jit(solution)/shard_map/ppermute | solution.py:289
  72.8 6.7 %copy-start.3 = (s32[32,16]{0,1:T(8,128)S(1)}, s32[32,16]{0,1:T(8,128)}, u32[]{:S(2)}) copy-start(s32[32,16]{0,1:T(8,128)} %param.26) | copy-start | bytes 6148
